TPU v7x, 256 devices: a whole 4x4x8 slice. The times are simulated.
256 devices in a mesh: wide: 64 (over z_hi, x, y, core), narrow: 4 (over z_lo).
Axes of the slice: x: 4, y: 4, z: 8 (z_hi: 2, z_lo: 4; z = z_hi * 4 + z_lo), core: 2. Of those that a mesh axis runs over, the one named last changes fastest.
Arguments:
- factor_rows: float32 [1, 4, 4, 64, 16, 1024], P(None, 'narrow', None, 'wide'), may hold values from -0.09375 to 0.09375
- load_vectors: float32 [1, 4, 1024, 128], P(None, 'narrow', 'wide'), may hold values from -6 to 6
- child_updates: float32 [4, 1, 4, 1024, 128], P('narrow', None, None, 'wide'), may hold values from -4 to 4
- block_inverses: float32 [4, 1024, 1024], P(None, 'wide'), may hold values from -1 to 2, as said below
Outputs:
- forward_solution: float32 [1, 4, 1024, 128], P(None, 'narrow', 'wide')
Inputs may be any that keep to these rules, and one draw needn't show every extreme that they name: Each block of block_inverses has a diagonal between 0.4 and 1.6.
All inputs are finite; a program needn't handle non-finite values.
Results may differ from a plain program's by a relative error of at most 0.0001.
Values sent between devices are 32-bit elements; how exact they have to be, the bound alone decides.
A program may use at most 64 MiB of HBM per device.

v0:
```python
import jax
import jax.numpy as jnp
from jax import lax
from jax.sharding import PartitionSpec as P


def from_root(shard, axis, root):
    mine = lax.axis_index(axis) == root
    return lax.psum(jnp.where(mine, shard, jnp.zeros_like(shard)), axis)


def body(factor_rows, load_vectors, child_updates, block_inverses):
    blocks_dev = factor_rows.shape[0]
    narrow_count = lax.axis_size("narrow")
    block_count = blocks_dev * narrow_count
    sub_rows = factor_rows.shape[4]
    block_width = factor_rows.shape[5]
    case_count = load_vectors.shape[3]
    my_lane = lax.axis_index("narrow")
    panel = factor_rows.reshape(blocks_dev, block_count, sub_rows, block_width)
    kid_sums = lax.psum_scatter(child_updates, "narrow", scatter_dimension=2, tiled=True)
    given_part = load_vectors.reshape(blocks_dev, sub_rows, case_count) - kid_sums.reshape(
        blocks_dev, sub_rows, case_count
    )
    solved = jnp.zeros((block_count, sub_rows, case_count), jnp.float32)
    held_sums = jnp.zeros((blocks_dev, block_width, case_count), jnp.float32)

    def advance(block_index, state_pair):
        solved, held_sums = state_pair
        own_block = block_index // narrow_count
        owner = block_index % narrow_count
        rows_here = lax.dynamic_index_in_dim(panel, own_block, 0, keepdims=False)
        reduced = lax.psum_scatter(
            jnp.einsum("cqr,cqk->rk", rows_here, solved, precision=lax.Precision.HIGHEST),
            "wide",
            scatter_dimension=0,
            tiled=True,
        )
        residual_part = lax.dynamic_index_in_dim(given_part, own_block, 0, keepdims=False) - reduced
        inverse_rows = lax.dynamic_index_in_dim(block_inverses, block_index, 0, keepdims=False)
        residual_full = lax.all_gather(residual_part, "wide", axis=0, tiled=True)
        applied = jnp.dot(
            inverse_rows,
            residual_full,
            precision=lax.Precision.HIGHEST,
            preferred_element_type=jnp.float32,
        )
        newest = from_root(applied, "narrow", owner)
        solved = lax.dynamic_update_index_in_dim(solved, newest, block_index, 0)
        return (solved, held_sums)

    solved, held_sums = lax.fori_loop(0, block_count, advance, (solved, held_sums))
    arranged = solved.reshape(blocks_dev, narrow_count, sub_rows, case_count)
    return lax.dynamic_slice_in_dim(arranged, my_lane, 1, 1)


def solution(mesh):
    placed = (
        P(None, "narrow", None, "wide", None, None),
        P(None, "narrow", "wide", None),
        P("narrow", None, None, "wide", None),
        P(None, "wide", None),
    )
    return jax.shard_map(
        body, mesh=mesh, in_specs=placed, out_specs=P(None, "narrow", "wide", None), check_vma=False
    )
```

profile of v0, /device:TPU:8, one launch (start us, length us, event | category | flops | bytes accessed | tf_op | source)
XLA Modules:
  0.0 2172.6 jit_solution(16757187029783483254)
XLA Ops:
  6.5 0.0 reduce-scatter.3.cloned.1.call-start
  6.5 0.7 reduce-scatter.3.cloned.1.call-update
  7.3 0.0 copy-start
  7.3 29.7 %reduce-scatter.3.cloned.1.call-done = f32[1,1,1,16,128]{4,3,2,1,0:T(8,128)} async-done(((f32[1,1,4,16,128]{4,3,2,1,0:T(8,128)}), f32[1,1,1,16,128]{4,3,2,1,0:T(8,128)}) %reduce-scatter.3.cloned.1.call-update) | async-done | bytes 8208 | tf_op jit(solution)/shard_map/reduce_scatter | solution.py:21
  36.9 0.0 copy-done
  36.9 0.7 bitcast_subtract_fusion.1
  37.6 2127.8 %while.15 = (s32[]{:T(128)}, f32[4,16,128]{2,1,0:T(8,128)S(1)}, f32[4,16,1024]{2,1,0:T(8,128)}, f32[1,16,128]{2,1,0:T(8,128)S(1)}, f32[1,4,16,1024]{3,2,1,0:T(8,...) while((s32[]{:T(128)}, f32[4,16,128]{2,1,0:T(8,128)S(1)}, f32[4,16,1024]{2,1,0:T(8,128)}, ...), condition=%wide.region_4.5_spmd, body=%wide.region_1.4_spmd.sunk | while | flops 125835264 | bytes 3604725 | solution.py:52
  37.6 0.0 reduce-scatter.5.cloned.1.call-start
  37.7 2.7 convolution_bitcast_fusion.2
  40.4 0.0 reduce-scatter.5.cloned.1.call-update
  40.4 401.7 %reduce-scatter.5.cloned.1.call-done = f32[16,128]{1,0:T(8,128)} async-done(((f32[1024,128]{1,0:T(8,128)}), f32[16,128]{1,0:T(8,128)}) %reduce-scatter.5.cloned.1.call-update) | async-done | bytes 8208 | tf_op jit(solution)/shard_map/while/body/eval_jaxpr/reduce_scatter | solution.py:33
  442.2 0.7 bitcast_subtract_fusion.3
  442.9 119.2 %all_gather.11 = f32[1024,128]{1,0:T(8,128)S(1)} all-gather(f32[16,128]{1,0:T(8,128)S(1)} %bitcast_subtract_fusion.3), channel_id=1, replica_groups=mesh['wide'=64,'narrow'=4] {'wide'}, dimensions={0}, use_global_device_ids=true | all-gather | bytes 532480 | tf_op jit(solution)/shard_map/while/body/eval_jaxpr/all_gather | solution.py:41
  562.0 1.2 fusion.16
  563.2 10.3 psum.15
  573.6 0.0 reduce-scatter.5.cloned.1.call-start
  573.6 2.7 convolution_bitcast_fusion.2
  576.4 0.0 reduce-scatter.5.cloned.1.call-update
  576.4 397.5 %reduce-scatter.5.cloned.1.call-done = f32[16,128]{1,0:T(8,128)} async-done(((f32[1024,128]{1,0:T(8,128)}), f32[16,128]{1,0:T(8,128)}) %reduce-scatter.5.cloned.1.call-update) | async-done | bytes 8208 | tf_op jit(solution)/shard_map/while/body/eval_jaxpr/reduce_scatter | solution.py:33
  973.9 0.7 bitcast_subtract_fusion.3
  974.6 119.1 %all_gather.11 = f32[1024,128]{1,0:T(8,128)S(1)} all-gather(f32[16,128]{1,0:T(8,128)S(1)} %bitcast_subtract_fusion.3), channel_id=1, replica_groups=mesh['wide'=64,'narrow'=4] {'wide'}, dimensions={0}, use_global_device_ids=true | all-gather | bytes 532480 | tf_op jit(solution)/shard_map/while/body/eval_jaxpr/all_gather | solution.py:41
  1093.8 1.2 fusion.16
  1095.0 9.3 psum.15
  1104.4 0.0 reduce-scatter.5.cloned.1.call-start
  1104.4 2.7 convolution_bitcast_fusion.2
  1107.1 0.0 reduce-scatter.5.cloned.1.call-update
  1107.2 397.3 %reduce-scatter.5.cloned.1.call-done = f32[16,128]{1,0:T(8,128)} async-done(((f32[1024,128]{1,0:T(8,128)}), f32[16,128]{1,0:T(8,128)}) %reduce-scatter.5.cloned.1.call-update) | async-done | bytes 8208 | tf_op jit(solution)/shard_map/while/body/eval_jaxpr/reduce_scatter | solution.py:33
  1504.5 0.7 bitcast_subtract_fusion.3
  1505.2 119.1 %all_gather.11 = f32[1024,128]{1,0:T(8,128)S(1)} all-gather(f32[16,128]{1,0:T(8,128)S(1)} %bitcast_subtract_fusion.3), channel_id=1, replica_groups=mesh['wide'=64,'narrow'=4] {'wide'}, dimensions={0}, use_global_device_ids=true | all-gather | bytes 532480 | tf_op jit(solution)/shard_map/while/body/eval_jaxpr/all_gather | solution.py:41
  1624.3 1.2 fusion.16
  1625.5 9.4 psum.15
  1634.9 0.0 reduce-scatter.5.cloned.1.call-start
  1635.0 2.7 convolution_bitcast_fusion.2
  1637.7 0.0 reduce-scatter.5.cloned.1.call-update
  1637.7 397.3 %reduce-scatter.5.cloned.1.call-done = f32[16,128]{1,0:T(8,128)} async-done(((f32[1024,128]{1,0:T(8,128)}), f32[16,128]{1,0:T(8,128)}) %reduce-scatter.5.cloned.1.call-update) | async-done | bytes 8208 | tf_op jit(solution)/shard_map/while/body/eval_jaxpr/reduce_scatter | solution.py:33
  2035.0 0.7 bitcast_subtract_fusion.3
  2035.7 119.1 %all_gather.11 = f32[1024,128]{1,0:T(8,128)S(1)} all-gather(f32[16,128]{1,0:T(8,128)S(1)} %bitcast_subtract_fusion.3), channel_id=1, replica_groups=mesh['wide'=64,'narrow'=4] {'wide'}, dimensions={0}, use_global_device_ids=true | all-gather | bytes 532480 | tf_op jit(solution)/shard_map/while/body/eval_jaxpr/all_gather | solution.py:41
  2154.8 1.2 fusion.16
  2156.1 9.3 psum.15
  2165.4 0.6 dynamic-slice_bitcast_fusion
  (5 shorter events, 0.0 us)
Async XLA Ops:
  6.5 30.4 %reduce-scatter.3.cloned.1.call-start = ((), (), s32[]{:S(2)}) async-start(), calls=%async_computation.2 | async-start | bytes 40960 | tf_op jit(solution)/shard_map/reduce_scatter | solution.py:21
  7.3 29.7 %copy-start = (f32[1,1,16,128]{3,2,1,0:T(8,128)S(1)}, f32[1,1,16,128]{3,2,1,0:T(8,128)}, u32[]{:S(2)}) copy-start(f32[1,1,16,128]{3,2,1,0:T(8,128)} %param.7) | copy-start | bytes 24580
  37.6 404.5 %reduce-scatter.5.cloned.1.call-start = ((), (), s32[]{:S(2)}) async-start(), calls=%async_computation.3 | async-start | bytes 532480 | tf_op jit(solution)/shard_map/while/body/eval_jaxpr/reduce_scatter | solution.py:33
  573.6 400.3 %reduce-scatter.5.cloned.1.call-start = ((), (), s32[]{:S(2)}) async-start(), calls=%async_computation.3 | async-start | bytes 532480 | tf_op jit(solution)/shard_map/while/body/eval_jaxpr/reduce_scatter | solution.py:33
  1104.4 400.1 %reduce-scatter.5.cloned.1.call-start = ((), (), s32[]{:S(2)}) async-start(), calls=%async_computation.3 | async-start | bytes 532480 | tf_op jit(solution)/shard_map/while/body/eval_jaxpr/reduce_scatter | solution.py:33
  1634.9 400.1 %reduce-scatter.5.cloned.1.call-start = ((), (), s32[]{:S(2)}) async-start(), calls=%async_computation.3 | async-start | bytes 532480 | tf_op jit(solution)/shard_map/while/body/eval_jaxpr/reduce_scatter | solution.py:33
Sparse Core Ops, SparseCore 0:
  9.8 27.0 reduce-scatter.2
  41.1 400.9 reduce-scatter.4
  577.0 396.8 reduce-scatter.4
  1107.5 396.8 reduce-scatter.4
  1638.1 396.8 reduce-scatter.4
where the time goes:
time: 2170 us
  waiting for transfers between devices  1620 us (75%)
  blocking collectives  515 us (24%)
    reduce_scatter x4, waiting for transfers between devices, advance(): lax.psum_scatter(jnp.einsum('cqr,cqk->rk', rows_here, solved, precision=l...  1590 us
    all_gather x4, blocking collectives, advance(): residual_full = lax.all_gather(residual_part, 'wide', axis=0, tiled=True)  477 us
  transfers between devices with their start and end apart: 5, of which 5 were waited for; matrix products, arithmetic and copies ran while one was open for 0% of the time, Pallas kernels for 0%

commit v1 on v0

--- a/solution.py
+++ b/solution.py
@@ -38,7 +38,9 @@
         )
         residual_part = lax.dynamic_index_in_dim(given_part, own_block, 0, keepdims=False) - reduced
         inverse_rows = lax.dynamic_index_in_dim(block_inverses, block_index, 0, keepdims=False)
-        residual_full = lax.all_gather(residual_part, "wide", axis=0, tiled=True)
+        residual_full = jnp.concatenate(
+            lax.all_to_all(jnp.stack([residual_part] * lax.axis_size("wide")), "wide", 0, 0), axis=0
+        )
         applied = jnp.dot(
             inverse_rows,
             residual_full,

time: 2170 us -> 1840 us (0.85)
  blocking collectives: 515 us -> 52.6 us
  waiting for transfers between devices: 1620 us -> 1690 us
  starting transfers between devices: 0.15 us -> 58.1 us
    all_gather x4 -> x0, blocking collectives: 477 us -> none  [advance(): residual_full = lax.all_gather(residual_part, 'wide', axis=0, tiled=True)]
    all_to_all x0 -> x4, waiting for transfers between devices: none -> 67.7 us  [advance(): lax.all_to_all(jnp.stack([residual_part] * lax.axis_size('wide')), 'wide'...]
    all_to_all x0 -> x4, starting transfers between devices: none -> 58 us  [advance(): lax.all_to_all(jnp.stack([residual_part] * lax.axis_size('wide')), 'wide'...]
  transfers between devices with their start and end apart: 5 -> 9, of which waited for: 5 -> 9; matrix products, arithmetic and copies ran while one was open for 0% -> 0% of each run, Pallas kernels for 0% -> 0%
where the time goes in v1:
time: 1840 us
  waiting for transfers between devices  1690 us (92%)
  starting transfers between devices  58.1 us (3%)
  blocking collectives  52.6 us (3%)
    reduce_scatter x4, waiting for transfers between devices, advance(): lax.psum_scatter(jnp.einsum('cqr,cqk->rk', rows_here, solved, precision=l...  1590 us
    all_to_all x4, waiting for transfers between devices, advance(): lax.all_to_all(jnp.stack([residual_part] * lax.axis_size('wide')), 'wide'...  67.7 us
    all_to_all x4, starting transfers between devices, advance(): lax.all_to_all(jnp.stack([residual_part] * lax.axis_size('wide')), 'wide'...  58 us
    psum x4, blocking collectives, from_root(): return lax.psum(jnp.where(mine, shard, jnp.zeros_like(shard)), axis)  52.6 us
  transfers between devices with their start and end apart: 9, of which 9 were waited for; matrix products, arithmetic and copies ran while one was open for 0% of the time, Pallas kernels for 0%

profile of v1, /device:TPU:8, one launch (start us, length us, event | category | flops | bytes accessed | tf_op | source)
XLA Modules:
  0.0 1838.2 jit_solution(3760407542793656174)
XLA Ops:
  6.5 0.0 reduce-scatter.3.cloned.1.call-start
  6.5 0.7 reduce-scatter.3.cloned.1.call-update
  7.3 0.0 copy-start
  7.3 29.7 %reduce-scatter.3.cloned.1.call-done = f32[1,1,1,16,128]{4,3,2,1,0:T(8,128)} async-done(((f32[1,1,4,16,128]{4,3,2,1,0:T(8,128)}), f32[1,1,1,16,128]{4,3,2,1,0:T(8,128)}) %reduce-scatter.3.cloned.1.call-update) | async-done | bytes 8208 | tf_op jit(solution)/shard_map/reduce_scatter | solution.py:21
  36.9 0.0 copy-done
  36.9 0.7 bitcast_subtract_fusion.1
  37.6 1793.4 %while.15 = (s32[]{:T(128)}, f32[4,16,128]{2,1,0:T(8,128)S(1)}, f32[4,16,1024]{2,1,0:T(8,128)}, f32[1,16,128]{2,1,0:T(8,128)S(1)}, f32[1,4,16,1024]{3,2,1,0:T(8,...) while((s32[]{:T(128)}, f32[4,16,128]{2,1,0:T(8,128)S(1)}, f32[4,16,1024]{2,1,0:T(8,128)}, ...), condition=%wide.region_4.5_spmd, body=%wide.region_1.4_spmd.sunk | while | flops 125835264 | bytes 5177621 | solution.py:54
  37.6 0.0 reduce-scatter.5.cloned.1.call-start
  37.7 2.7 convolution_bitcast_fusion.2
  40.4 0.0 reduce-scatter.5.cloned.1.call-update
  40.4 401.7 %reduce-scatter.5.cloned.1.call-done = f32[16,128]{1,0:T(8,128)} async-done(((f32[1024,128]{1,0:T(8,128)}), f32[16,128]{1,0:T(8,128)}) %reduce-scatter.5.cloned.1.call-update) | async-done | bytes 8208 | tf_op jit(solution)/shard_map/while/body/eval_jaxpr/reduce_scatter | solution.py:33
  442.2 0.7 bitcast_subtract_fusion.3
  442.9 0.8 stack.7
  443.7 14.5 all-to-all-start
  458.2 16.5 all-to-all-done
  474.6 1.2 fusion.16
  475.8 13.3 psum.15
  489.2 0.0 reduce-scatter.5.cloned.1.call-start
  489.3 2.7 convolution_bitcast_fusion.2
  492.0 0.0 reduce-scatter.5.cloned.1.call-update
  492.0 397.5 %reduce-scatter.5.cloned.1.call-done = f32[16,128]{1,0:T(8,128)} async-done(((f32[1024,128]{1,0:T(8,128)}), f32[16,128]{1,0:T(8,128)}) %reduce-scatter.5.cloned.1.call-update) | async-done | bytes 8208 | tf_op jit(solution)/shard_map/while/body/eval_jaxpr/reduce_scatter | solution.py:33
  889.5 0.7 bitcast_subtract_fusion.3
  890.2 0.8 stack.7
  891.0 14.5 all-to-all-start
  905.6 17.1 all-to-all-done
  922.7 1.2 fusion.16
  923.9 12.8 psum.15
  936.7 0.0 reduce-scatter.5.cloned.1.call-start
  936.8 2.7 convolution_bitcast_fusion.2
  939.5 0.0 reduce-scatter.5.cloned.1.call-update
  939.5 397.1 %reduce-scatter.5.cloned.1.call-done = f32[16,128]{1,0:T(8,128)} async-done(((f32[1024,128]{1,0:T(8,128)}), f32[16,128]{1,0:T(8,128)}) %reduce-scatter.5.cloned.1.call-update) | async-done | bytes 8208 | tf_op jit(solution)/shard_map/while/body/eval_jaxpr/reduce_scatter | solution.py:33
  1336.6 0.7 bitcast_subtract_fusion.3
  1337.3 0.8 stack.7
  1338.1 14.5 all-to-all-start
  1352.6 17.1 all-to-all-done
  1369.8 1.2 fusion.16
  1371.0 12.9 psum.15
  1383.9 0.0 reduce-scatter.5.cloned.1.call-start
  1384.0 2.7 convolution_bitcast_fusion.2
  1386.7 0.0 reduce-scatter.5.cloned.1.call-update
  1386.7 396.5 %reduce-scatter.5.cloned.1.call-done = f32[16,128]{1,0:T(8,128)} async-done(((f32[1024,128]{1,0:T(8,128)}), f32[16,128]{1,0:T(8,128)}) %reduce-scatter.5.cloned.1.call-update) | async-done | bytes 8208 | tf_op jit(solution)/shard_map/while/body/eval_jaxpr/reduce_scatter | solution.py:33
  1783.2 0.7 bitcast_subtract_fusion.3
  1783.9 0.8 stack.7
  1784.8 14.5 all-to-all-start
  1799.2 17.0 all-to-all-done
  1816.2 1.2 fusion.16
  1817.4 13.6 psum.15
  1831.1 0.6 dynamic-slice_bitcast_fusion
  (5 shorter events, 0.0 us)
Async XLA Ops:
  6.5 30.4 %reduce-scatter.3.cloned.1.call-start = ((), (), s32[]{:S(2)}) async-start(), calls=%async_computation.3 | async-start | bytes 40960 | tf_op jit(solution)/shard_map/reduce_scatter | solution.py:21
  7.3 29.7 %copy-start = (f32[1,1,16,128]{3,2,1,0:T(8,128)S(1)}, f32[1,1,16,128]{3,2,1,0:T(8,128)}, u32[]{:S(2)}) copy-start(f32[1,1,16,128]{3,2,1,0:T(8,128)} %param.7) | copy-start | bytes 24580
  37.6 404.5 %reduce-scatter.5.cloned.1.call-start = ((), (), s32[]{:S(2)}) async-start(), calls=%async_computation.4 | async-start | bytes 532480 | tf_op jit(solution)/shard_map/while/body/eval_jaxpr/reduce_scatter | solution.py:33
  443.7 31.0 %all-to-all-start = ((f32[64,16,128]{2,1,0:T(8,128)}), f32[64,16,128]{2,1,0:T(8,128)S(1)}, u32[]{:S(2)}, u32[]{:S(2)}) async-start(f32[64,16,128]{2,1,0:T(8,128)} %stack.7), calls=%async_computation.1 | async-start | bytes 1048576 | tf_op jit(solution)/shard_map/while/body/eval_jaxpr/all_to_all | solution.py:42
  489.2 400.3 %reduce-scatter.5.cloned.1.call-start = ((), (), s32[]{:S(2)}) async-start(), calls=%async_computation.4 | async-start | bytes 532480 | tf_op jit(solution)/shard_map/while/body/eval_jaxpr/reduce_scatter | solution.py:33
  891.0 31.6 %all-to-all-start = ((f32[64,16,128]{2,1,0:T(8,128)}), f32[64,16,128]{2,1,0:T(8,128)S(1)}, u32[]{:S(2)}, u32[]{:S(2)}) async-start(f32[64,16,128]{2,1,0:T(8,128)} %stack.7), calls=%async_computation.1 | async-start | bytes 1048576 | tf_op jit(solution)/shard_map/while/body/eval_jaxpr/all_to_all | solution.py:42
  936.7 399.9 %reduce-scatter.5.cloned.1.call-start = ((), (), s32[]{:S(2)}) async-start(), calls=%async_computation.4 | async-start | bytes 532480 | tf_op jit(solution)/shard_map/while/body/eval_jaxpr/reduce_scatter | solution.py:33
  1338.1 31.7 %all-to-all-start = ((f32[64,16,128]{2,1,0:T(8,128)}), f32[64,16,128]{2,1,0:T(8,128)S(1)}, u32[]{:S(2)}, u32[]{:S(2)}) async-start(f32[64,16,128]{2,1,0:T(8,128)} %stack.7), calls=%async_computation.1 | async-start | bytes 1048576 | tf_op jit(solution)/shard_map/while/body/eval_jaxpr/all_to_all | solution.py:42
  1383.9 399.3 %reduce-scatter.5.cloned.1.call-start = ((), (), s32[]{:S(2)}) async-start(), calls=%async_computation.4 | async-start | bytes 532480 | tf_op jit(solution)/shard_map/while/body/eval_jaxpr/reduce_scatter | solution.py:33
  1784.8 31.4 %all-to-all-start = ((f32[64,16,128]{2,1,0:T(8,128)}), f32[64,16,128]{2,1,0:T(8,128)S(1)}, u32[]{:S(2)}, u32[]{:S(2)}) async-start(f32[64,16,128]{2,1,0:T(8,128)} %stack.7), calls=%async_computation.1 | async-start | bytes 1048576 | tf_op jit(solution)/shard_map/while/body/eval_jaxpr/all_to_all | solution.py:42
Sparse Core Ops, SparseCore 0:
  9.8 27.0 reduce-scatter.2
  41.1 400.9 reduce-scatter.4
  492.7 396.7 reduce-scatter.4
  939.9 396.6 reduce-scatter.4
  1387.1 396.1 reduce-scatter.4
